TPU v7x, 32 devices: a whole 2x2x4 slice. The times are simulated.
32 devices in a mesh: dap: 8 (over y, x, core), dp: 4 (over z).
Axes of the slice: x: 2, y: 2, z: 4, core: 2. Of those that a mesh axis runs over, the one named last changes fastest.
Arguments:
- family_matrix: bfloat16 [512, 32, 256], P(('dp', 'dap')), parts along dimension 0, may hold values from -6 to 6
- edge_matrix: bfloat16 [128, 32, 128], P(('dp', 'dap')), parts along dimension 0, may hold values from -6 to 6
- edge_validity: int32 [128, 32], P(('dp', 'dap')), parts along dimension 0, may hold values 0 or 1
- query_key_value_gate_matrix: bfloat16 [256, 1024], replicated, may hold values from -0.375 to 0.375
- logit_offset_matrix: bfloat16 [128, 8], replicated, as said below
- heads_merge_matrix: bfloat16 [256, 256], replicated, may hold values from -0.375 to 0.375
- left_right_factor_matrix: bfloat16 [256, 64], replicated, may hold values from -0.375 to 0.375
- covariance_merge_matrix: bfloat16 [1024, 128], replicated, may hold values from -1 to 1
- edges_gate_factor_matrix: bfloat16 [128, 384], replicated, may hold values from -0.5 to 0.5
- cycle_merge_matrix: bfloat16 [128, 128], replicated, may hold values from -0.5 to 0.5
- loss_sensitivity: bfloat16 [128, 32, 128], P(('dp', 'dap')), parts along dimension 0, may hold values from -6 to 6
Outputs:
- family_after_heads: bfloat16 [512, 32, 256], P(('dp', 'dap')), parts along dimension 0
- pair_output: bfloat16 [128, 32, 128], P(('dp', 'dap')), parts along dimension 0
- pair_gradient: float32 [128, 32, 128], P(('dp', 'dap')), parts along dimension 0
There are 4 independent parts, one for each index of `dp`. A program takes and returns all parts, laid end to end along the dimension named above; an argument that names none is the same for every part. Nothing has to cross between parts.
Inputs may be any that keep to these rules, and one draw needn't show every extreme that they name: `logit_offset_matrix`: independent entries of a fixed spread clipped at four deviations.
All inputs are finite; a program needn't handle non-finite values. No bound on the sum of `edge_validity` on one device may be relied on, other than what follows from the above.
Results may differ from a plain program's by a relative error of at most 0.02.
Values may be sent and summed in bfloat16 or wider, within the bound.
No kernel may reach another device: no remote copies, remote signals or barrier semaphores. Data moves between devices by JAX's collectives and lax.ppermute only.
A program may use at most 64 MiB of HBM per device.

v0:
```python
import math
import jax
import jax.numpy as jnp
from jax import lax
from jax.sharding import PartitionSpec as P

EPSILON = 1e-05


def standardize_features(values):
    center = values - jnp.mean(values, -1, keepdims=True)
    scale_inv = lax.rsqrt(jnp.mean(center * center, -1, keepdims=True) + EPSILON)
    return center * scale_inv


def norm_back(values, grad_out):
    center = values - jnp.mean(values, -1, keepdims=True)
    scale_inv = lax.rsqrt(jnp.mean(center * center, -1, keepdims=True) + EPSILON)
    standardized_source = center * scale_inv
    return scale_inv * (
        grad_out
        - jnp.mean(grad_out, -1, keepdims=True)
        - standardized_source * jnp.mean(grad_out * standardized_source, -1, keepdims=True)
    )


def lateral_heads_mixing(
    family_shard_slice, logit_offset_whole, query_key_value_gate_matrix, heads_merge_matrix
):
    homolog_number, amino_number, feature_depth = family_shard_slice.shape
    head_count = logit_offset_whole.shape[1]
    head_size = feature_depth // head_count
    standardized_source = standardize_features(family_shard_slice.astype(jnp.float32)).astype(
        jnp.bfloat16
    )
    projected = jnp.dot(
        standardized_source.reshape(-1, feature_depth),
        query_key_value_gate_matrix,
        preferred_element_type=jnp.float32,
    )
    projected = projected.reshape(homolog_number, amino_number, 4 * feature_depth)
    shape_heads = (homolog_number, amino_number, head_count, head_size)
    queries = projected[..., :feature_depth].astype(jnp.bfloat16).reshape(shape_heads)
    key_rows = (
        projected[..., feature_depth : 2 * feature_depth].astype(jnp.bfloat16).reshape(shape_heads)
    )
    value_rows = (
        projected[..., 2 * feature_depth : 3 * feature_depth]
        .astype(jnp.bfloat16)
        .reshape(shape_heads)
    )
    gating = jax.nn.sigmoid(projected[..., 3 * feature_depth :])
    logits = jnp.einsum("sihd,sjhd->sihj", queries, key_rows, preferred_element_type=jnp.float32)
    logits = logits / math.sqrt(head_size) + logit_offset_whole.astype(jnp.float32)[None]
    weights = jax.nn.softmax(logits, axis=-1).astype(jnp.bfloat16)
    mixed = jnp.einsum("sihj,sjhd->sihd", weights, value_rows, preferred_element_type=jnp.float32)
    gated = (gating * mixed.reshape(homolog_number, amino_number, feature_depth)).astype(
        jnp.bfloat16
    )
    edge_increment = jnp.dot(
        gated.reshape(-1, feature_depth), heads_merge_matrix, preferred_element_type=jnp.float32
    )
    return (
        family_shard_slice.astype(jnp.float32)
        + edge_increment.reshape(homolog_number, amino_number, feature_depth)
    ).astype(jnp.bfloat16)


def pair_projection_step(alignment_rows, left_right_factor_matrix):
    standardized_source = standardize_features(alignment_rows.astype(jnp.float32)).astype(
        jnp.bfloat16
    )
    edge_result = jnp.dot(
        standardized_source.reshape(-1, alignment_rows.shape[2]),
        left_right_factor_matrix,
        preferred_element_type=jnp.float32,
    )
    return edge_result.reshape(alignment_rows.shape[0], alignment_rows.shape[1], -1).astype(
        jnp.bfloat16
    )


def body(
    family_matrix,
    edge_matrix,
    edge_validity,
    query_key_value_gate_matrix,
    logit_offset_matrix,
    heads_merge_matrix,
    left_right_factor_matrix,
    covariance_merge_matrix,
    edges_gate_factor_matrix,
    cycle_merge_matrix,
    loss_sensitivity,
):
    res_rows, width, pair_chans = edge_matrix.shape
    pair_normed = standardize_features(edge_matrix.astype(jnp.float32)).astype(jnp.bfloat16)
    bias_local = jnp.einsum(
        "ijc,ch->ihj", pair_normed, logit_offset_matrix, preferred_element_type=jnp.float32
    ).astype(jnp.bfloat16)
    logit_offset_whole = lax.all_gather(bias_local, "dap", axis=0, tiled=True)
    homolog_lines = family_matrix.shape[0]
    homolog_subset = math.gcd(homolog_lines, 8)
    batched_lines = family_matrix.reshape(
        homolog_lines // homolog_subset,
        homolog_subset,
        family_matrix.shape[1],
        family_matrix.shape[2],
    )
    family_after_heads = lax.map(
        lambda family_shard_slice: lateral_heads_mixing(
            family_shard_slice, logit_offset_whole, query_key_value_gate_matrix, heads_merge_matrix
        ),
        batched_lines,
    ).reshape(family_matrix.shape)
    hidden = left_right_factor_matrix.shape[1] // 2
    weight_f32 = covariance_merge_matrix.astype(jnp.float32)
    alignment_columns = lax.all_to_all(
        family_after_heads, "dap", split_axis=1, concat_axis=0, tiled=True
    )
    edge_result = pair_projection_step(alignment_columns, left_right_factor_matrix)
    left_part = edge_result[..., :hidden]
    right_part = edge_result[..., hidden:]
    sequence_full_count = alignment_columns.shape[0]
    shard_in = lax.all_gather(right_part, "dap", axis=1, tiled=True)
    outer_sum = (
        jnp.einsum("sia,sjb->ijab", left_part, shard_in, preferred_element_type=jnp.float32)
        / sequence_full_count
    )
    row_count = shard_in.shape[1]
    flat = outer_sum.reshape(res_rows * row_count, hidden * hidden)
    edge_increment = jnp.dot(flat, weight_f32, precision=lax.Precision.HIGHEST).reshape(
        res_rows, row_count, pair_chans
    )
    pair_mid = (edge_matrix.astype(jnp.float32) + edge_increment).astype(jnp.bfloat16)
    tri_normed = standardize_features(pair_mid.astype(jnp.float32)).astype(jnp.bfloat16)
    tri_proj = jnp.dot(
        tri_normed.reshape(-1, pair_chans),
        edges_gate_factor_matrix,
        preferred_element_type=jnp.float32,
    ).reshape(res_rows, width, 3 * pair_chans)
    mask_f = edge_validity.astype(jnp.float32)[..., None]
    side_a = (mask_f * tri_proj[..., :pair_chans]).astype(jnp.bfloat16)
    side_b = (mask_f * tri_proj[..., pair_chans : 2 * pair_chans]).astype(jnp.bfloat16)
    gating = jax.nn.sigmoid(tri_proj[..., 2 * pair_chans :])
    tri_prod = jnp.einsum(
        "ikc,jkc->ijc",
        side_a,
        lax.all_gather(side_b, "dap", axis=0, tiled=True),
        preferred_element_type=jnp.float32,
    )
    prod_normed = standardize_features(tri_prod).astype(jnp.bfloat16)
    tri_update = jnp.dot(
        prod_normed.reshape(-1, pair_chans), cycle_merge_matrix, preferred_element_type=jnp.float32
    ).reshape(res_rows, width, pair_chans)
    pair_output = (pair_mid.astype(jnp.float32) + gating * tri_update).astype(jnp.bfloat16)
    cot_f32 = loss_sensitivity.astype(jnp.float32)
    grad_update = (cot_f32 * gating).astype(jnp.bfloat16)
    grad_normed = jnp.dot(
        grad_update.reshape(-1, pair_chans),
        cycle_merge_matrix.T,
        preferred_element_type=jnp.float32,
    ).reshape(res_rows, width, pair_chans)
    grad_prod = norm_back(tri_prod, grad_normed).astype(jnp.bfloat16)
    grad_part = grad_prod
    grad_a = jnp.einsum(
        "ijc,jkc->ikc",
        grad_part,
        lax.all_gather(side_b, "dap", axis=0, tiled=True),
        preferred_element_type=jnp.float32,
    )
    grad_part = grad_prod
    grad_b = lax.psum_scatter(
        jnp.einsum("ijc,ikc->jkc", grad_part, side_a, preferred_element_type=jnp.float32).astype(
            jnp.bfloat16
        ),
        "dap",
        scatter_dimension=0,
        tiled=True,
    ).astype(jnp.float32)
    grad_gate = cot_f32 * tri_update * gating * (1.0 - gating)
    grad_proj = jnp.concatenate([mask_f * grad_a, mask_f * grad_b, grad_gate], -1).astype(
        jnp.bfloat16
    )
    grad_input = jnp.dot(
        grad_proj.reshape(-1, 3 * pair_chans),
        edges_gate_factor_matrix.T,
        preferred_element_type=jnp.float32,
    ).reshape(res_rows, width, pair_chans)
    pair_gradient = cot_f32 + norm_back(pair_mid.astype(jnp.float32), grad_input)
    return (family_after_heads, pair_output, pair_gradient)


def solution(mesh):
    in_specs = (
        P(("dp", "dap"), None, None),
        P(("dp", "dap"), None, None),
        P(("dp", "dap"), None),
        P(),
        P(),
        P(),
        P(),
        P(),
        P(),
        P(),
        P(("dp", "dap"), None, None),
    )
    out_specs = (
        P(("dp", "dap"), None, None),
        P(("dp", "dap"), None, None),
        P(("dp", "dap"), None, None),
    )
    return jax.shard_map(body, mesh=mesh, in_specs=in_specs, out_specs=out_specs, check_vma=False)
```

profile of v0, /device:TPU:0, one launch (start us, length us, event | category | flops | bytes accessed | tf_op | source)
XLA Modules:
  0.0 126.4 jit_solution(6555764046027350197)
XLA Ops:
  7.2 0.9 convert_reduce_fusion.1
  8.1 0.9 fusion.56
  9.0 1.0 fusion.36
  10.0 10.7 %all_gather.10 = bf16[32,8,32]{2,1,0:T(8,128)(2,1)S(1)} all-gather(bf16[4,8,32]{2,1,0:T(8,128)(2,1)S(1)} %fusion.36), channel_id=1, replica_groups=mesh['dap'=8,'dp'=4] {'dap'}, dimensions={0}, use_global_device_ids=true | all-gather | bytes 18432 | tf_op jit(solution)/shard_map/all_gather | solution.py:101
  20.8 20.3 %while.10 = (s32[]{:T(128)}, bf16[2,8,32,256]{3,2,1,0:T(8,128)(2,1)}, bf16[2,8,32,256]{3,2,1,0:T(8,128)(2,1)}, bf16[256,1024]{1,0:T(8,128)(2,1)}, bf16[32,8,32]{...) while((s32[]{:T(128)}, bf16[2,8,32,256]{3,2,1,0:T(8,128)(2,1)}, ...), condition=%wide.region_7.8_spmd, body=%wide.region_2.7_spmd.sunk | while | flops 178071872 | bytes 7186573 | solution.py:110
  20.9 1.0 convert_reduce_fusion.3
  21.9 1.1 fusion.126
  23.0 1.5 %fusion.127 = (bf16[8,32,1024]{2,1,0:T(8,128)(2,1)S(1)}, f32[8,32,1024]{2,1,0:T(8,128)S(1)}) fusion(bf16[256,1024]{1,0:T(8,128)(2,1)} %get-tuple-element.193, f32[8,32]{1,0:T(8,128)S(1)} %add_rsqrt_fusion.5, f32[8,32]{1,0:T(8,128)S(1)} %broadcast_multiply_fusion.9, bf16[2,8,32,256]{3,2,1,0:T(8,128)(2,1)} %get-tuple-element.192, s32[]{:T(128)} %get-tuple-element.183), kind=kOutput, calls=%fused_computation.130.clone.1 | convolution fusion | flops 134742016 | bytes 2230784 | tf_op jit(solution)/shard_map/while/body/eval_jaxpr/dot_general | solution.py:36
  24.5 0.2 reshape.216
  24.8 0.2 reshape.217
  25.1 0.4 fusion.129
  25.5 0.9 fusion.130
  26.4 1.0 copy.176
  27.4 1.4 %fusion.131 = f32[8,8,32,32]{3,2,1,0:T(8,128)S(1)} fusion(bf16[8,32,8,32]{1,3,2,0:T(8,128)(2,1)} %bitcast.148, f32[8,32,8]{1,2,0:T(8,128)} %fusion.130, f32[8,32,8,32]{1,3,2,0:T(8,128)S(1)} %fusion.129), kind=kOutput, calls=%fused_computation.11.clone.1 | convolution fusion | flops 4392991 | bytes 663552 | tf_op jit(solution)/shard_map/while/body/eval_jaxpr/sihj,sjhd->sihd/dot_general | solution.py:56
  28.8 0.3 copy.177
  29.1 1.8 %fusion.132 = bf16[2,8,32,256]{3,2,1,0:T(8,128)(2,1)} fusion(bf16[2,8,32,256]{3,2,1,0:T(8,128)(2,1)} %get-tuple-element.184, s32[]{:T(128)} %get-tuple-element.183, f32[8,32,256]{2,1,0:T(8,128)S(1)} %copy.177, f32[8,32,1024]{2,1,0:T(8,128)S(1)} %get-tuple-element.175, bf16[256,256]{1,0:T(8,128)(2,1)} %get-tuple-element.195, ...), kind=kOutput, calls=%fused_computation.9.clone.1 | convolution fusion | flops 34078720 | bytes 918016 | tf_op jit(solution)/shard_map/while/body/eval_jaxpr/dot_general | solution.py:60
  31.0 1.0 convert_reduce_fusion.3
  32.0 1.1 fusion.126
  33.2 1.5 %fusion.127 = (bf16[8,32,1024]{2,1,0:T(8,128)(2,1)S(1)}, f32[8,32,1024]{2,1,0:T(8,128)S(1)}) fusion(bf16[256,1024]{1,0:T(8,128)(2,1)} %get-tuple-element.193, f32[8,32]{1,0:T(8,128)S(1)} %add_rsqrt_fusion.5, f32[8,32]{1,0:T(8,128)S(1)} %broadcast_multiply_fusion.9, bf16[2,8,32,256]{3,2,1,0:T(8,128)(2,1)} %get-tuple-element.192, s32[]{:T(128)} %get-tuple-element.183), kind=kOutput, calls=%fused_computation.130.clone.1 | convolution fusion | flops 134742016 | bytes 2230784 | tf_op jit(solution)/shard_map/while/body/eval_jaxpr/dot_general | solution.py:36
  34.7 0.2 reshape.216
  34.9 0.2 reshape.217
  35.2 0.4 fusion.129
  35.6 0.9 fusion.130
  36.5 1.0 copy.176
  37.5 1.4 %fusion.131 = f32[8,8,32,32]{3,2,1,0:T(8,128)S(1)} fusion(bf16[8,32,8,32]{1,3,2,0:T(8,128)(2,1)} %bitcast.148, f32[8,32,8]{1,2,0:T(8,128)} %fusion.130, f32[8,32,8,32]{1,3,2,0:T(8,128)S(1)} %fusion.129), kind=kOutput, calls=%fused_computation.11.clone.1 | convolution fusion | flops 4392991 | bytes 663552 | tf_op jit(solution)/shard_map/while/body/eval_jaxpr/sihj,sjhd->sihd/dot_general | solution.py:56
  39.0 0.3 copy.177
  39.3 1.8 %fusion.132 = bf16[2,8,32,256]{3,2,1,0:T(8,128)(2,1)} fusion(bf16[2,8,32,256]{3,2,1,0:T(8,128)(2,1)} %get-tuple-element.184, s32[]{:T(128)} %get-tuple-element.183, f32[8,32,256]{2,1,0:T(8,128)S(1)} %copy.177, f32[8,32,1024]{2,1,0:T(8,128)S(1)} %get-tuple-element.175, bf16[256,256]{1,0:T(8,128)(2,1)} %get-tuple-element.195, ...), kind=kOutput, calls=%fused_computation.9.clone.1 | convolution fusion | flops 34078720 | bytes 918016 | tf_op jit(solution)/shard_map/while/body/eval_jaxpr/dot_general | solution.py:60
  41.1 1.8 %copy.169 = bf16[2,8,32,256]{3,1,0,2:T(8,128)(2,1)} copy(bf16[2,8,32,256]{3,2,1,0:T(8,128)(2,1)} %get-tuple-element.35) | data formatting | bytes 524288 | tf_op jit(solution)/shard_map/while | solution.py:110
  42.9 3.4 %all-to-all-start = ((bf16[16,32,256]{2,0,1:T(8,128)(2,1)}), bf16[16,32,256]{2,0,1:T(8,128)(2,1)S(1)}, u32[]{:S(2)}, u32[]{:S(2)}) async-start(bf16[16,32,256]{2,0,1:T(8,128)(2,1)} %bitcast.121), calls=%async_computation | async-start | bytes 524288 | tf_op jit(solution)/shard_map/all_to_all | solution.py:118
  46.4 6.8 %all-to-all-done = bf16[16,32,256]{2,0,1:T(8,128)(2,1)S(1)} async-done(((bf16[16,32,256]{2,0,1:T(8,128)(2,1)}), bf16[16,32,256]{2,0,1:T(8,128)(2,1)S(1)}, u32[]{:S(2)}, u32[]{:S(2)}) %all-to-all-start) | async-done | bytes 262176 | tf_op jit(solution)/shard_map/all_to_all | solution.py:118
  53.5 0.3 multiply_reduce_fusion
  54.4 8.4 %all_gather.11 = bf16[128,32,32]{0,2,1:T(8,128)(2,1)S(1)} all-gather(bf16[128,4,32]{0,2,1:T(8,128)(2,1)S(1)} %slice.39), channel_id=1, replica_groups=mesh['dap'=8,'dp'=4] {'dap'}, dimensions={1}, use_global_device_ids=true | all-gather | bytes 294912 | tf_op jit(solution)/shard_map/all_gather | solution.py:125
  62.7 1.8 %multiply_bitcast_fusion = f32[4,32,32,32]{2,3,0,1:T(8,128)} fusion(bf16[128,32,32]{0,2,1:T(8,128)(2,1)S(1)} %all_gather.11, bf16[128,4,64]{0,2,1:T(8,128)(2,1)S(1)} %convolution_convert_fusion), kind=kOutput, calls=%fused_computation.40 | convolution fusion | flops 33685504 | bytes 819200 | tf_op jit(solution)/shard_map/sia,sjb->ijab/dot_general | solution.py:127
  64.5 1.9 %copy.138 = f32[4,32,32,32]{3,2,1,0:T(8,128)S(1)} copy(f32[4,32,32,32]{2,3,0,1:T(8,128)} %multiply_bitcast_fusion) | data formatting | bytes 1048576 | tf_op jit(solution)/shard_map/div | solution.py:127
  66.5 1.0 dot_general.50
  67.5 0.5 fusion.89
  68.5 9.5 %all_gather.12 = bf16[32,32,128]{2,1,0:T(8,128)(2,1)S(1)} all-gather(bf16[4,32,128]{2,1,0:T(8,128)(2,1)S(1)} %get-tuple-element.117), channel_id=1, replica_groups=mesh['dap'=8,'dp'=4] {'dap'}, dimensions={0}, use_global_device_ids=true | all-gather | bytes 294912 | tf_op jit(solution)/shard_map/all_gather | solution.py:149
  77.9 1.4 %copy.139 = bf16[32,32,128]{1,0,2:T(8,128)(2,1)S(1)} copy(bf16[32,32,128]{2,1,0:T(8,128)(2,1)S(1)} %all_gather.12) | data formatting | bytes 524288 | tf_op jit(solution)/shard_map/all_gather | solution.py:149
  79.5 0.7 fusion.90
  80.2 0.2 fusion.91
  81.1 0.5 fusion.93
  81.6 2.0 %copy.147 = bf16[128,32,32]{0,1,2:T(8,128)(2,1)} copy(bf16[128,32,32]{2,1,0:T(8,128)(2,1)S(1)} %fusion.93) | data formatting | bytes 524288 | tf_op jit(solution)/shard_map/ijc,ikc->jkc/dot_general | solution.py:174
  83.6 0.4 fusion.92
  84.1 0.8 fusion.61
  84.9 32.7 %reduce-scatter.2.cloned.1.call-done = bf16[4,32,128]{2,1,0:T(8,128)(2,1)} async-done(((bf16[32,32,128]{2,1,0:T(8,128)(2,1)}), bf16[4,32,128]{2,1,0:T(8,128)(2,1)}) %reduce-scatter.2.cloned.1.call-update) | async-done | bytes 32784 | tf_op jit(solution)/shard_map/reduce_scatter | solution.py:173
  117.6 0.8 fusion.67
  118.5 0.3 fusion.85
  118.8 0.8 convert_add_fusion
  (64 shorter events, 2.5 us)
Async XLA Ops:
  7.2 60.3 %copy-start = (bf16[1024,128]{1,0:T(8,128)(2,1)S(1)}, bf16[1024,128]{1,0:T(8,128)(2,1)}, u32[]{:S(2)}) copy-start(bf16[1024,128]{1,0:T(8,128)(2,1)} %param.20) | copy-start | bytes 786436
  20.8 25.6 %copy-start.7 = (s32[4,32]{1,0:T(4,128)S(1)}, s32[4,32]{1,0:T(4,128)}, u32[]{:S(2)}) copy-start(s32[4,32]{1,0:T(4,128)} %param.15) | copy-start | bytes 1540
  20.8 4.2 %copy-start.1 = (bf16[32,8,32]{0,2,1:T(8,128)(2,1)}, bf16[32,8,32]{0,2,1:T(8,128)(2,1)S(1)}, u32[]{:S(2)}) copy-start(bf16[32,8,32]{0,2,1:T(8,128)(2,1)S(1)} %get-tuple-element.194) | copy-start | bytes 49156 | tf_op jit(solution)/shard_map/while
  28.8 2.2 %copy-start.2 = (bf16[32,8,32]{0,2,1:T(8,128)(2,1)S(1)}, bf16[32,8,32]{0,2,1:T(8,128)(2,1)}, u32[]{:S(2)}) copy-start(bf16[32,8,32]{0,2,1:T(8,128)(2,1)} %copy-done.1) | copy-start | bytes 49156 | tf_op jit(solution)/shard_map/while
  31.0 4.2 %copy-start.1 = (bf16[32,8,32]{0,2,1:T(8,128)(2,1)}, bf16[32,8,32]{0,2,1:T(8,128)(2,1)S(1)}, u32[]{:S(2)}) copy-start(bf16[32,8,32]{0,2,1:T(8,128)(2,1)S(1)} %get-tuple-element.194) | copy-start | bytes 49156 | tf_op jit(solution)/shard_map/while
  39.0 2.2 %copy-start.2 = (bf16[32,8,32]{0,2,1:T(8,128)(2,1)S(1)}, bf16[32,8,32]{0,2,1:T(8,128)(2,1)}, u32[]{:S(2)}) copy-start(bf16[32,8,32]{0,2,1:T(8,128)(2,1)} %copy-done.1) | copy-start | bytes 49156 | tf_op jit(solution)/shard_map/while
  41.1 13.0 %copy-start.5 = (bf16[256,64]{0,1:T(8,128)(2,1)S(1)}, bf16[256,64]{0,1:T(8,128)(2,1)}, u32[]{:S(2)}) copy-start(bf16[256,64]{0,1:T(8,128)(2,1)} %param.19) | copy-start | bytes 98308
  42.9 10.3 %all-to-all-start = ((bf16[16,32,256]{2,0,1:T(8,128)(2,1)}), bf16[16,32,256]{2,0,1:T(8,128)(2,1)S(1)}, u32[]{:S(2)}, u32[]{:S(2)}) async-start(bf16[16,32,256]{2,0,1:T(8,128)(2,1)} %bitcast.121), calls=%async_computation | async-start | bytes 524288 | tf_op jit(solution)/shard_map/all_to_all | solution.py:118
  46.3 71.3 %reduce-scatter.2.cloned.1.call-start = ((), (), s32[]{:S(2)}) async-start(), calls=%async_computation.2 | async-start | bytes 294912 | tf_op jit(solution)/shard_map/reduce_scatter | solution.py:173
  66.5 1.0 copy-start.3
  66.5 1.6 %copy-start.4 = (bf16[128,384]{1,0:T(8,128)(2,1)S(1)}, bf16[128,384]{1,0:T(8,128)(2,1)}, u32[]{:S(2)}) copy-start(bf16[128,384]{1,0:T(8,128)(2,1)} %param.21) | copy-start | bytes 294916
  67.9 12.3 %copy-start.6 = (bf16[4,32,128]{2,1,0:T(8,128)(2,1)S(1)}, bf16[4,32,128]{2,1,0:T(8,128)(2,1)}, u32[]{:S(2)}) copy-start(bf16[4,32,128]{2,1,0:T(8,128)(2,1)} %param.23) | copy-start | bytes 98308
  67.9 12.3 %copy-start.8 = (bf16[128,128]{1,0:T(8,128)(2,1)S(1)}, bf16[128,128]{1,0:T(8,128)(2,1)}, u32[]{:S(2)}) copy-start(bf16[128,128]{1,0:T(8,128)(2,1)} %param.22) | copy-start | bytes 98308
Sparse Core Ops, SparseCore 0:
  83.7 33.8 reduce-scatter.1
where the time goes:
time: 127 us; the launch traced here: 126 us
  waiting for transfers between devices  39.5 us (31%)
  blocking collectives  28.5 us (22%)
  matrix products  16.8 us (13%)
  between operations  14.3 us (11%)
  local copies, waits for them, and re-layouts  12.5 us (10%)
  other arithmetic  11 us (9%)
  starting transfers between devices  3.45 us (3%)
    reduce_scatter x1, waiting for transfers between devices, body(): lax.psum_scatter(jnp.einsum('ijc,ikc->jkc', grad_part, side_a, preferred_...  32.7 us
    all_gather x1, blocking collectives, body(): logit_offset_whole = lax.all_gather(bias_local, 'dap', axis=0, tiled=True)  10.7 us
    all_gather x1, blocking collectives, body(): lax.all_gather(side_b, 'dap', axis=0, tiled=True)  9.47 us
    all_gather x1, blocking collectives, body(): shard_in = lax.all_gather(right_part, 'dap', axis=1, tiled=True)  8.35 us
    all_to_all x1, waiting for transfers between devices, body(): lax.all_to_all(family_after_heads, 'dap', split_axis=1, concat_axis=0, ti...  6.8 us
    dot_general x2, matrix products, lateral_heads_mixing(): jnp.dot(gated.reshape(-1, feature_depth), heads_merge_matrix, preferred_e...  3.69 us
    reduce_sum x6, other arithmetic, standardize_features(): jnp.mean(center * center, -1, keepdims=True) + EPSILON  3.67 us
    all_to_all x1, starting transfers between devices, body(): lax.all_to_all(family_after_heads, 'dap', split_axis=1, concat_axis=0, ti...  3.41 us
  transfers between devices with their start and end apart: 2, of which 2 were waited for; matrix products, arithmetic and copies ran while one was open for 1% of the time, Pallas kernels for 0%

commit v1 on v0

--- a/solution.py
+++ b/solution.py
@@ -5,6 +5,28 @@
 from jax.sharding import PartitionSpec as P
 
 EPSILON = 1e-05
+
+
+def in_order(parts, dim):
+    shape = list(parts.shape[1:])
+    shape[dim] *= parts.shape[0]
+    return jnp.moveaxis(parts, 0, dim).reshape(shape)
+
+
+def gather_around(x, axis, dim):
+    count = lax.axis_size(axis)
+    pairs = [(i, (i + 1) % count) for i in range(count)]
+    back = [(b, a) for a, b in pairs]
+    lower, upper = ([], [])
+    for step in range(count - 1):
+        if step % 2 == 0:
+            lower.append(lax.ppermute(lower[-1] if lower else x, axis, pairs))
+        else:
+            upper.append(lax.ppermute(upper[-1] if upper else x, axis, back))
+    blocks = jnp.stack([*lower[::-1], x, *upper])
+    shift = lax.axis_index(axis) - len(lower)
+    blocks = blocks[(jnp.arange(count) - shift) % count]
+    return in_order(blocks, dim)
 
 
 def standardize_features(values):
@@ -144,10 +166,7 @@
     side_b = (mask_f * tri_proj[..., pair_chans : 2 * pair_chans]).astype(jnp.bfloat16)
     gating = jax.nn.sigmoid(tri_proj[..., 2 * pair_chans :])
     tri_prod = jnp.einsum(
-        "ikc,jkc->ijc",
-        side_a,
-        lax.all_gather(side_b, "dap", axis=0, tiled=True),
-        preferred_element_type=jnp.float32,
+        "ikc,jkc->ijc", side_a, gather_around(side_b, "dap", 0), preferred_element_type=jnp.float32
     )
     prod_normed = standardize_features(tri_prod).astype(jnp.bfloat16)
     tri_update = jnp.dot(

time: 127 us -> 146 us (1.15)
  waiting for transfers between devices: 39.5 us -> 49 us
  starting transfers between devices: 3.45 us -> 10.8 us
  local copies, waits for them, and re-layouts: 12.5 us -> 14.6 us
    ppermute x0 -> x7, waiting for transfers between devices: none -> 8.27 us  [the longest x4 6.76 us: gather_around(): lower.append(lax.ppermute(lower[-1] if lower else x, axis, pairs))]
    ppermute x0 -> x7, starting transfers between devices: none -> 7.39 us  [the longest x3 6.98 us: gather_around(): upper.append(lax.ppermute(upper[-1] if upper else x, axis, back))]
  transfers between devices with their start and end apart: 2 -> 9, of which waited for: 2 -> 6; matrix products, arithmetic and copies ran while one was open for 1% -> 2% of each run, Pallas kernels for 0% -> 0%
where the time goes in v1:
time: 146 us; the launch traced here: 145 us
  waiting for transfers between devices  49 us (34%)
  blocking collectives  28.4 us (19%)
  matrix products  16.8 us (12%)
  local copies, waits for them, and re-layouts  14.6 us (10%)
  between operations  14.4 us (10%)
  other arithmetic  11 us (8%)
  starting transfers between devices  10.8 us (7%)
    reduce_scatter x1, waiting for transfers between devices, body(): lax.psum_scatter(jnp.einsum('ijc,ikc->jkc', grad_part, side_a, preferred_...  33.9 us
    all_gather x1, blocking collectives, body(): logit_offset_whole = lax.all_gather(bias_local, 'dap', axis=0, tiled=True)  10.7 us
    all_gather x1, blocking collectives, body(): lax.all_gather(side_b, 'dap', axis=0, tiled=True)  9.35 us
    all_gather x1, blocking collectives, body(): shard_in = lax.all_gather(right_part, 'dap', axis=1, tiled=True)  8.35 us
    ppermute x3, starting transfers between devices, gather_around(): upper.append(lax.ppermute(upper[-1] if upper else x, axis, back))  6.98 us
    all_to_all x1, waiting for transfers between devices, body(): lax.all_to_all(family_after_heads, 'dap', split_axis=1, concat_axis=0, ti...  6.79 us
    ppermute x4, waiting for transfers between devices, gather_around(): lower.append(lax.ppermute(lower[-1] if lower else x, axis, pairs))  6.76 us
    dot_general x2, matrix products, lateral_heads_mixing(): jnp.dot(gated.reshape(-1, feature_depth), heads_merge_matrix, preferred_e...  3.69 us
  transfers between devices with their start and end apart: 9, of which 6 were waited for; matrix products, arithmetic and copies ran while one was open for 2% of the time, Pallas kernels for 0%

profile of v1, /device:TPU:0, one launch (start us, length us, event | category | flops | bytes accessed | tf_op | source)
XLA Modules:
  0.0 145.4 jit_solution(12423252072178044105)
XLA Ops:
  7.2 0.9 convert_reduce_fusion.1
  8.1 0.9 fusion.56
  9.0 1.0 fusion.36
  10.0 10.7 %all_gather.9 = bf16[32,8,32]{2,1,0:T(8,128)(2,1)S(1)} all-gather(bf16[4,8,32]{2,1,0:T(8,128)(2,1)S(1)} %fusion.36), channel_id=1, replica_groups=mesh['dap'=8,'dp'=4] {'dap'}, dimensions={0}, use_global_device_ids=true | all-gather | bytes 18432 | tf_op jit(solution)/shard_map/all_gather | solution.py:123
  20.8 20.3 %while.10 = (s32[]{:T(128)}, bf16[2,8,32,256]{3,2,1,0:T(8,128)(2,1)}, bf16[2,8,32,256]{3,2,1,0:T(8,128)(2,1)}, bf16[256,1024]{1,0:T(8,128)(2,1)}, bf16[32,8,32]{...) while((s32[]{:T(128)}, bf16[2,8,32,256]{3,2,1,0:T(8,128)(2,1)}, ...), condition=%wide.region_7.8_spmd, body=%wide.region_2.7_spmd.sunk | while | flops 178071872 | bytes 7186573 | solution.py:132
  20.9 1.0 convert_reduce_fusion.3
  21.9 1.1 fusion.128
  23.0 1.5 %fusion.129 = (bf16[8,32,1024]{2,1,0:T(8,128)(2,1)S(1)}, f32[8,32,1024]{2,1,0:T(8,128)S(1)}) fusion(bf16[256,1024]{1,0:T(8,128)(2,1)} %get-tuple-element.193, f32[8,32]{1,0:T(8,128)S(1)} %add_rsqrt_fusion.5, f32[8,32]{1,0:T(8,128)S(1)} %broadcast_multiply_fusion.9, bf16[2,8,32,256]{3,2,1,0:T(8,128)(2,1)} %get-tuple-element.192, s32[]{:T(128)} %get-tuple-element.183), kind=kOutput, calls=%fused_computation.146.clone.1 | convolution fusion | flops 134742016 | bytes 2230784 | tf_op jit(solution)/shard_map/while/body/eval_jaxpr/dot_general | solution.py:58
  25.1 0.4 fusion.131
  25.5 0.9 fusion.132
  26.4 1.0 copy.176
  27.4 1.4 fusion.133
  29.1 1.8 %fusion.134 = bf16[2,8,32,256]{3,2,1,0:T(8,128)(2,1)} fusion(bf16[2,8,32,256]{3,2,1,0:T(8,128)(2,1)} %get-tuple-element.184, s32[]{:T(128)} %get-tuple-element.183, f32[8,32,256]{2,1,0:T(8,128)S(1)} %copy.177, f32[8,32,1024]{2,1,0:T(8,128)S(1)} %get-tuple-element.175, bf16[256,256]{1,0:T(8,128)(2,1)} %get-tuple-element.195, ...), kind=kOutput, calls=%fused_computation.10.clone.1 | convolution fusion | flops 34078720 | bytes 918016 | tf_op jit(solution)/shard_map/while/body/eval_jaxpr/dot_general | solution.py:82
  31.0 1.0 convert_reduce_fusion.3
  32.0 1.1 fusion.128
  33.2 1.5 %fusion.129 = (bf16[8,32,1024]{2,1,0:T(8,128)(2,1)S(1)}, f32[8,32,1024]{2,1,0:T(8,128)S(1)}) fusion(bf16[256,1024]{1,0:T(8,128)(2,1)} %get-tuple-element.193, f32[8,32]{1,0:T(8,128)S(1)} %add_rsqrt_fusion.5, f32[8,32]{1,0:T(8,128)S(1)} %broadcast_multiply_fusion.9, bf16[2,8,32,256]{3,2,1,0:T(8,128)(2,1)} %get-tuple-element.192, s32[]{:T(128)} %get-tuple-element.183), kind=kOutput, calls=%fused_computation.146.clone.1 | convolution fusion | flops 134742016 | bytes 2230784 | tf_op jit(solution)/shard_map/while/body/eval_jaxpr/dot_general | solution.py:58
  35.2 0.4 fusion.131
  35.6 0.9 fusion.132
  36.5 1.0 copy.176
  37.5 1.4 fusion.133
  39.3 1.8 %fusion.134 = bf16[2,8,32,256]{3,2,1,0:T(8,128)(2,1)} fusion(bf16[2,8,32,256]{3,2,1,0:T(8,128)(2,1)} %get-tuple-element.184, s32[]{:T(128)} %get-tuple-element.183, f32[8,32,256]{2,1,0:T(8,128)S(1)} %copy.177, f32[8,32,1024]{2,1,0:T(8,128)S(1)} %get-tuple-element.175, bf16[256,256]{1,0:T(8,128)(2,1)} %get-tuple-element.195, ...), kind=kOutput, calls=%fused_computation.10.clone.1 | convolution fusion | flops 34078720 | bytes 918016 | tf_op jit(solution)/shard_map/while/body/eval_jaxpr/dot_general | solution.py:82
  41.1 1.8 %copy.169 = bf16[2,8,32,256]{3,1,0,2:T(8,128)(2,1)} copy(bf16[2,8,32,256]{3,2,1,0:T(8,128)(2,1)} %get-tuple-element.35) | data formatting | bytes 524288 | tf_op jit(solution)/shard_map/while | solution.py:132
  42.9 3.4 %all-to-all-start = ((bf16[16,32,256]{2,0,1:T(8,128)(2,1)}), bf16[16,32,256]{2,0,1:T(8,128)(2,1)S(1)}, u32[]{:S(2)}, u32[]{:S(2)}) async-start(bf16[16,32,256]{2,0,1:T(8,128)(2,1)} %bitcast.140), calls=%async_computation | async-start | bytes 524288 | tf_op jit(solution)/shard_map/all_to_all | solution.py:140
  46.4 6.8 %all-to-all-done = bf16[16,32,256]{2,0,1:T(8,128)(2,1)S(1)} async-done(((bf16[16,32,256]{2,0,1:T(8,128)(2,1)}), bf16[16,32,256]{2,0,1:T(8,128)(2,1)S(1)}, u32[]{:S(2)}, u32[]{:S(2)}) %all-to-all-start) | async-done | bytes 262176 | tf_op jit(solution)/shard_map/all_to_all | solution.py:140
  54.4 8.4 %all_gather.10 = bf16[128,32,32]{0,2,1:T(8,128)(2,1)S(1)} all-gather(bf16[128,4,32]{0,2,1:T(8,128)(2,1)S(1)} %slice.41), channel_id=1, replica_groups=mesh['dap'=8,'dp'=4] {'dap'}, dimensions={1}, use_global_device_ids=true | all-gather | bytes 294912 | tf_op jit(solution)/shard_map/all_gather | solution.py:147
  62.7 1.8 %multiply_bitcast_fusion = f32[4,32,32,32]{2,3,0,1:T(8,128)} fusion(bf16[128,32,32]{0,2,1:T(8,128)(2,1)S(1)} %all_gather.10, bf16[128,4,64]{0,2,1:T(8,128)(2,1)S(1)} %convolution_convert_fusion), kind=kOutput, calls=%fused_computation.41 | convolution fusion | flops 33685504 | bytes 819200 | tf_op jit(solution)/shard_map/sia,sjb->ijab/dot_general | solution.py:149
  64.5 1.9 %copy.138 = f32[4,32,32,32]{3,2,1,0:T(8,128)S(1)} copy(f32[4,32,32,32]{2,3,0,1:T(8,128)} %multiply_bitcast_fusion) | data formatting | bytes 1048576 | tf_op jit(solution)/shard_map/div | solution.py:149
  66.5 1.0 dot_general.50
  67.5 0.5 fusion.91
  68.5 0.4 collective-permute-start
  68.9 3.9 %collective-permute-done = bf16[4,32,128]{2,1,0:T(8,128)(2,1)S(1)} collective-permute-done((bf16[4,32,128]{2,1,0:T(8,128)(2,1)S(1)}, bf16[4,32,128]{2,1,0:T(8,128)(2,1)S(1)}, u32[]{:S(2)}, u32[]{:S(2)}) %collective-permute-start) | collective-permute-done | bytes 32800 | tf_op jit(solution)/shard_map/ppermute | solution.py:23
  72.8 2.6 %collective-permute-start.4 = (bf16[4,32,128]{2,1,0:T(8,128)(2,1)S(1)}, bf16[4,32,128]{2,1,0:T(8,128)(2,1)S(1)}, u32[]{:S(2)}, u32[]{:S(2)}) collective-permute-start(bf16[4,32,128]{2,1,0:T(8,128)(2,1)S(1)} %get-tuple-element.117), channel_id=1, source_target_pairs={{4,0},{8,4},{12,8},{16,12},{20,16},{24,20},{28,24},{0,28},{5,1},{9... | collective-permute-start | bytes 98312 | tf_op jit(solution)/shard_map/ppermute | solution.py:25
  75.4 1.9 %collective-permute-done.1 = bf16[4,32,128]{2,1,0:T(8,128)(2,1)S(1)} collective-permute-done((bf16[4,32,128]{2,1,0:T(8,128)(2,1)S(1)}, bf16[4,32,128]{2,1,0:T(8,128)(2,1)S(1)}, u32[]{:S(2)}, u32[]{:S(2)}) %collective-permute-start.1) | collective-permute-done | bytes 32800 | tf_op jit(solution)/shard_map/ppermute | solution.py:23
  77.9 2.7 %collective-permute-start.5 = (bf16[4,32,128]{2,1,0:T(8,128)(2,1)S(1)}, bf16[4,32,128]{2,1,0:T(8,128)(2,1)S(1)}, u32[]{:S(2)}, u32[]{:S(2)}) collective-permute-start(bf16[4,32,128]{2,1,0:T(8,128)(2,1)S(1)} %collective-permute-done.4), channel_id=1, source_target_pairs={{4,0},{8,4},{12,8},{16,12},{20,16},{24,20},{28,24},{0,28},{5,1},{9... | collective-permute-start | bytes 98312 | tf_op jit(solution)/shard_map/ppermute | solution.py:25
  80.6 1.0 collective-permute-done.2
  81.6 9.4 %all_gather.11 = bf16[32,32,128]{2,1,0:T(8,128)(2,1)S(1)} all-gather(bf16[4,32,128]{2,1,0:T(8,128)(2,1)S(1)} %get-tuple-element.117), channel_id=1, replica_groups=mesh['dap'=8,'dp'=4] {'dap'}, dimensions={0}, use_global_device_ids=true | all-gather | bytes 294912 | tf_op jit(solution)/shard_map/all_gather | solution.py:188
  90.9 1.4 copy.144
  92.4 1.6 %collective-permute-start.6 = (bf16[4,32,128]{2,1,0:T(8,128)(2,1)S(1)}, bf16[4,32,128]{2,1,0:T(8,128)(2,1)S(1)}, u32[]{:S(2)}, u32[]{:S(2)}) collective-permute-start(bf16[4,32,128]{2,1,0:T(8,128)(2,1)S(1)} %collective-permute-done.5), channel_id=1, source_target_pairs={{4,0},{8,4},{12,8},{16,12},{20,16},{24,20},{28,24},{0,28},{5,1},{9... | collective-permute-start | bytes 98312 | tf_op jit(solution)/shard_map/ppermute | solution.py:25
  94.1 1.5 %collective-permute-done.6 = bf16[4,32,128]{2,1,0:T(8,128)(2,1)S(1)} collective-permute-done((bf16[4,32,128]{2,1,0:T(8,128)(2,1)S(1)}, bf16[4,32,128]{2,1,0:T(8,128)(2,1)S(1)}, u32[]{:S(2)}, u32[]{:S(2)}) %collective-permute-start.6) | collective-permute-done | bytes 32800 | tf_op jit(solution)/shard_map/ppermute | solution.py:25
  95.6 0.6 gather_fusion
  96.2 1.4 copy.139
  97.7 0.7 fusion.92
  98.8 0.5 fusion.95
  99.3 2.0 %copy.147 = bf16[128,32,32]{0,1,2:T(8,128)(2,1)} copy(bf16[128,32,32]{2,1,0:T(8,128)(2,1)S(1)} %fusion.95) | data formatting | bytes 524288 | tf_op jit(solution)/shard_map/ijc,ikc->jkc/dot_general | solution.py:193
  101.8 0.8 fusion.61
  102.7 33.9 %reduce-scatter.2.cloned.1.call-done = bf16[4,32,128]{2,1,0:T(8,128)(2,1)} async-done(((bf16[32,32,128]{2,1,0:T(8,128)(2,1)}), bf16[4,32,128]{2,1,0:T(8,128)(2,1)}) %reduce-scatter.2.cloned.1.call-update) | async-done | bytes 32784 | tf_op jit(solution)/shard_map/reduce_scatter | solution.py:192
  136.6 0.8 fusion.67
  137.7 0.8 convert_add_fusion
  (90 shorter events, 5.4 us)
Async XLA Ops:
  7.2 60.3 %copy-start = (bf16[1024,128]{1,0:T(8,128)(2,1)S(1)}, bf16[1024,128]{1,0:T(8,128)(2,1)}, u32[]{:S(2)}) copy-start(bf16[1024,128]{1,0:T(8,128)(2,1)} %param.20) | copy-start | bytes 786436
  20.8 25.6 %copy-start.7 = (s32[4,32]{1,0:T(4,128)S(1)}, s32[4,32]{1,0:T(4,128)}, u32[]{:S(2)}) copy-start(s32[4,32]{1,0:T(4,128)} %param.15) | copy-start | bytes 1540
  20.8 4.2 %copy-start.1 = (bf16[32,8,32]{0,2,1:T(8,128)(2,1)}, bf16[32,8,32]{0,2,1:T(8,128)(2,1)S(1)}, u32[]{:S(2)}) copy-start(bf16[32,8,32]{0,2,1:T(8,128)(2,1)S(1)} %get-tuple-element.194) | copy-start | bytes 49156 | tf_op jit(solution)/shard_map/while
  28.8 2.2 %copy-start.2 = (bf16[32,8,32]{0,2,1:T(8,128)(2,1)S(1)}, bf16[32,8,32]{0,2,1:T(8,128)(2,1)}, u32[]{:S(2)}) copy-start(bf16[32,8,32]{0,2,1:T(8,128)(2,1)} %copy-done.1) | copy-start | bytes 49156 | tf_op jit(solution)/shard_map/while
  31.0 4.2 %copy-start.1 = (bf16[32,8,32]{0,2,1:T(8,128)(2,1)}, bf16[32,8,32]{0,2,1:T(8,128)(2,1)S(1)}, u32[]{:S(2)}) copy-start(bf16[32,8,32]{0,2,1:T(8,128)(2,1)S(1)} %get-tuple-element.194) | copy-start | bytes 49156 | tf_op jit(solution)/shard_map/while
  39.0 2.2 %copy-start.2 = (bf16[32,8,32]{0,2,1:T(8,128)(2,1)S(1)}, bf16[32,8,32]{0,2,1:T(8,128)(2,1)}, u32[]{:S(2)}) copy-start(bf16[32,8,32]{0,2,1:T(8,128)(2,1)} %copy-done.1) | copy-start | bytes 49156 | tf_op jit(solution)/shard_map/while
  41.1 13.0 %copy-start.5 = (bf16[256,64]{0,1:T(8,128)(2,1)S(1)}, bf16[256,64]{0,1:T(8,128)(2,1)}, u32[]{:S(2)}) copy-start(bf16[256,64]{0,1:T(8,128)(2,1)} %param.19) | copy-start | bytes 98308
  42.9 10.3 %all-to-all-start = ((bf16[16,32,256]{2,0,1:T(8,128)(2,1)}), bf16[16,32,256]{2,0,1:T(8,128)(2,1)S(1)}, u32[]{:S(2)}, u32[]{:S(2)}) async-start(bf16[16,32,256]{2,0,1:T(8,128)(2,1)} %bitcast.140), calls=%async_computation | async-start | bytes 524288 | tf_op jit(solution)/shard_map/all_to_all | solution.py:140
  46.3 90.3 %reduce-scatter.2.cloned.1.call-start = ((), (), s32[]{:S(2)}) async-start(), calls=%async_computation.2 | async-start | bytes 294912 | tf_op jit(solution)/shard_map/reduce_scatter | solution.py:192
  66.5 1.0 copy-start.3
  66.5 1.7 %copy-start.4 = (bf16[128,384]{1,0:T(8,128)(2,1)S(1)}, bf16[128,384]{1,0:T(8,128)(2,1)}, u32[]{:S(2)}) copy-start(bf16[128,384]{1,0:T(8,128)(2,1)} %param.21) | copy-start | bytes 294916
  66.5 10.8 %copy-start.6 = (bf16[4,32,128]{2,1,0:T(8,128)(2,1)S(1)}, bf16[4,32,128]{2,1,0:T(8,128)(2,1)}, u32[]{:S(2)}) copy-start(bf16[4,32,128]{2,1,0:T(8,128)(2,1)} %param.23) | copy-start | bytes 98308
  66.5 10.8 %copy-start.8 = (bf16[128,128]{1,0:T(8,128)(2,1)S(1)}, bf16[128,128]{1,0:T(8,128)(2,1)}, u32[]{:S(2)}) copy-start(bf16[128,128]{1,0:T(8,128)(2,1)} %param.22) | copy-start | bytes 98308
  68.5 4.3 %collective-permute-start = (bf16[4,32,128]{2,1,0:T(8,128)(2,1)S(1)}, bf16[4,32,128]{2,1,0:T(8,128)(2,1)S(1)}, u32[]{:S(2)}, u32[]{:S(2)}) collective-permute-start(bf16[4,32,128]{2,1,0:T(8,128)(2,1)S(1)} %get-tuple-element.117), channel_id=1, source_target_pairs={{0,4},{4,8},{8,12},{12,16},{16,20},{20,24},{24,28},{28,0},{1,5},{5... | collective-permute-start | bytes 98312 | tf_op jit(solution)/shard_map/ppermute | solution.py:23
  72.8 4.6 %collective-permute-start.1 = (bf16[4,32,128]{2,1,0:T(8,128)(2,1)S(1)}, bf16[4,32,128]{2,1,0:T(8,128)(2,1)S(1)}, u32[]{:S(2)}, u32[]{:S(2)}) collective-permute-start(bf16[4,32,128]{2,1,0:T(8,128)(2,1)S(1)} %collective-permute-done), channel_id=1, source_target_pairs={{0,4},{4,8},{8,12},{12,16},{16,20},{20,24},{24,28},{28,0},{1,5},{5... | collective-permute-start | bytes 98312 | tf_op jit(solution)/shard_map/ppermute | solution.py:23
  72.8 5.1 %collective-permute-start.4 = (bf16[4,32,128]{2,1,0:T(8,128)(2,1)S(1)}, bf16[4,32,128]{2,1,0:T(8,128)(2,1)S(1)}, u32[]{:S(2)}, u32[]{:S(2)}) collective-permute-start(bf16[4,32,128]{2,1,0:T(8,128)(2,1)S(1)} %get-tuple-element.117), channel_id=1, source_target_pairs={{4,0},{8,4},{12,8},{16,12},{20,16},{24,20},{28,24},{0,28},{5,1},{9... | collective-permute-start | bytes 98312 | tf_op jit(solution)/shard_map/ppermute | solution.py:25
  77.3 4.2 %collective-permute-start.2 = (bf16[4,32,128]{2,1,0:T(8,128)(2,1)S(1)}, bf16[4,32,128]{2,1,0:T(8,128)(2,1)S(1)}, u32[]{:S(2)}, u32[]{:S(2)}) collective-permute-start(bf16[4,32,128]{2,1,0:T(8,128)(2,1)S(1)} %collective-permute-done.1), channel_id=1, source_target_pairs={{0,4},{4,8},{8,12},{12,16},{16,20},{20,24},{24,28},{28,0},{1,5},{5... | collective-permute-start | bytes 98312 | tf_op jit(solution)/shard_map/ppermute | solution.py:23
  77.9 14.5 %collective-permute-start.5 = (bf16[4,32,128]{2,1,0:T(8,128)(2,1)S(1)}, bf16[4,32,128]{2,1,0:T(8,128)(2,1)S(1)}, u32[]{:S(2)}, u32[]{:S(2)}) collective-permute-start(bf16[4,32,128]{2,1,0:T(8,128)(2,1)S(1)} %collective-permute-done.4), channel_id=1, source_target_pairs={{4,0},{8,4},{12,8},{16,12},{20,16},{24,20},{28,24},{0,28},{5,1},{9... | collective-permute-start | bytes 98312 | tf_op jit(solution)/shard_map/ppermute | solution.py:25
  81.6 12.5 %collective-permute-start.3 = (bf16[4,32,128]{2,1,0:T(8,128)(2,1)S(1)}, bf16[4,32,128]{2,1,0:T(8,128)(2,1)S(1)}, u32[]{:S(2)}, u32[]{:S(2)}) collective-permute-start(bf16[4,32,128]{2,1,0:T(8,128)(2,1)S(1)} %collective-permute-done.2), channel_id=1, source_target_pairs={{0,4},{4,8},{8,12},{12,16},{16,20},{20,24},{24,28},{28,0},{1,5},{5... | collective-permute-start | bytes 98312 | tf_op jit(solution)/shard_map/ppermute | solution.py:23
  92.4 3.2 %collective-permute-start.6 = (bf16[4,32,128]{2,1,0:T(8,128)(2,1)S(1)}, bf16[4,32,128]{2,1,0:T(8,128)(2,1)S(1)}, u32[]{:S(2)}, u32[]{:S(2)}) collective-permute-start(bf16[4,32,128]{2,1,0:T(8,128)(2,1)S(1)} %collective-permute-done.5), channel_id=1, source_target_pairs={{4,0},{8,4},{12,8},{16,12},{20,16},{24,20},{28,24},{0,28},{5,1},{9... | collective-permute-start | bytes 98312 | tf_op jit(solution)/shard_map/ppermute | solution.py:25
Sparse Core Ops, SparseCore 0:
  101.5 35.0 reduce-scatter.1
